TPU v7x, 128 devices: a whole 4x4x4 slice. The times are simulated.
128 devices in a mesh: tiles: 64 (over y, z_hi, x, core), vec: 2 (over z_lo).
Axes of the slice: x: 4, y: 4, z: 4 (z_hi: 2, z_lo: 2; z = z_hi * 2 + z_lo), core: 2. Of those that a mesh axis runs over, the one named last changes fastest.
Arguments:
- omega: float32 [128, 4, 512, 128], P('vec', None, 'tiles'), may hold values from -24 to 24
- conductance: float32 [3, 4, 512, 128], P(None, None, 'tiles'), may hold values from 0.02 to 0.16
- wet: int32 [512, 128], P('tiles'), may hold values 0 or 1
- volume: float32 [512, 128], P('tiles'), may hold values from 0.3 to 27, as said below
- face_runs: int32 [64, 4], P('tiles'), may hold values from 0 to 128, as said below
Outputs:
- diffused: float32 [128, 4, 512, 128], P('vec', None, 'tiles')
- r_factor: float32 [128, 128], replicated
Inputs may be any that keep to these rules, and one draw needn't show every extreme that they name: `face_runs`: tiles in tile row 0 have a closed lower row face and tiles in tile column 0 a closed lower column face (length 0); every other run lies within its face, covers at least half of it, and some tiles have fully open faces. Positive cell volume weights.
All inputs are finite; a program needn't handle non-finite values. No bound on the sum of `wet` on one device may be relied on, other than what follows from the above.
Results may differ from a plain program's by a relative error of at most 0.00005.
Values sent between devices are 32-bit elements; how exact they have to be, the bound alone decides.
A program may use at most 64 MiB of HBM per device.

v0:
```python
import jax
import jax.numpy as jnp
from jax import lax
from jax.sharding import PartitionSpec as P

TGY = 8
ITERS = 4


def shifted(value, axis, steps):
    count = lax.axis_size(axis)
    first, last = (max(0, -steps), min(count, count - steps))
    return lax.ppermute(value, axis, [(source, source + steps) for source in range(first, last)])


def diffuse(field, statics):
    cond_x = statics[0]
    cond_y = statics[1]
    cond_z = statics[2]
    wet_cells = statics[3]
    flux_x = cond_x[:, 1:, :] * (field[:, :, 1:, :] - field[:, :, :-1, :])
    flux_y = cond_y[:, :, 1:] * (field[:, :, :, 1:] - field[:, :, :, :-1])
    flux_z = cond_z[1:] * (field[:, 1:] - field[:, :-1])
    zero_level = jnp.zeros_like(field[:, :1])
    flux_z = jnp.concatenate([zero_level, flux_z, zero_level], axis=1)
    change = flux_x[:, :, 1:, 1:-1] - flux_x[:, :, :-1, 1:-1]
    change = change + flux_y[:, :, 1:-1, 1:] - flux_y[:, :, 1:-1, :-1]
    change = change + (flux_z[:, 1:] - flux_z[:, :-1])[:, :, 1:-1, 1:-1]
    return wet_cells[:, 1:-1, 1:-1] * (field[:, :, 1:-1, 1:-1] + change)


def moving(values, offset):
    return shifted(values, "tiles", offset)


def fixed_rim(values, offset):
    return shifted(values, "tiles", offset)


def extend(values, margin, neighbour):
    lower_rim = neighbour(values[:, :, -margin:, :], TGY)
    upper_rim = neighbour(values[:, :, :margin, :], -TGY)
    stacked = jnp.concatenate([lower_rim, values, upper_rim], axis=2)
    left_rim = neighbour(stacked[:, :, :, -margin:], 1)
    right_rim = neighbour(stacked[:, :, :, :margin], -1)
    return jnp.concatenate([left_rim, stacked, right_rim], axis=3)


def shards(omega, conductance, wet, volume, face_runs):
    levels = omega.shape[1]
    tile_rows = omega.shape[2]
    tile_cols = omega.shape[3]
    row_ids = lax.broadcasted_iota(jnp.int32, (tile_rows, tile_cols), 0)
    col_ids = lax.broadcasted_iota(jnp.int32, (tile_rows, tile_cols), 1)
    runs = face_runs[0]
    open_x = (col_ids >= runs[0]) & (col_ids < runs[0] + runs[1])
    factor_x = jnp.where(row_ids == 0, open_x.astype(jnp.float32), jnp.float32(1.0))
    open_y = (row_ids >= runs[2]) & (row_ids < runs[2] + runs[3])
    factor_y = jnp.where(col_ids == 0, open_y.astype(jnp.float32), jnp.float32(1.0))
    level_ids = lax.broadcasted_iota(jnp.int32, (levels, 1, 1), 0)
    cond_z = conductance[2] * (level_ids > 0).astype(jnp.float32)
    wet_float = wet.astype(jnp.float32)
    statics = jnp.stack(
        [
            conductance[0] * factor_x[None],
            conductance[1] * factor_y[None],
            cond_z,
            jnp.broadcast_to(wet_float[None], (levels, tile_rows, tile_cols)),
        ]
    )
    margin = 1
    statics_wide = extend(statics, margin, fixed_rim)
    field = wet_float[None, None] * omega
    for block_index in range(ITERS // margin):
        grown = extend(field, margin, moving)
        current = statics_wide
        grown = diffuse(grown, current)
        current = current[:, :, 1:-1, 1:-1]
        field = grown
    regrouped = lax.all_to_all(field, "vec", split_axis=1, concat_axis=0, tiled=True)
    all_vectors = regrouped.shape[0]
    total_cells = levels * lax.axis_size("tiles") * tile_rows * tile_cols
    flat_values = regrouped.reshape(all_vectors, -1)
    weighted = (regrouped * volume[None, None]).reshape(all_vectors, -1)
    gram_local = (
        lax.dot_general(
            weighted,
            flat_values,
            (((1,), (1,)), ((), ())),
            precision=lax.Precision.HIGHEST,
            preferred_element_type=jnp.float32,
        )
        / total_cells
    )
    gram = lax.psum(gram_local, ("tiles", "vec"))
    r_factor = jnp.linalg.cholesky(gram).T
    return (field, r_factor)


def solution(mesh):
    in_specs = (
        P("vec", None, "tiles", None),
        P(None, None, "tiles", None),
        P("tiles", None),
        P("tiles", None),
        P("tiles", None),
    )
    out_specs = (P("vec", None, "tiles", None), P())
    return jax.shard_map(shards, mesh=mesh, in_specs=in_specs, out_specs=out_specs, check_vma=False)
```

profile of v0, /device:TPU:1, one launch (start us, length us, event | category | flops | bytes accessed | tf_op | source)
XLA Modules:
  0.0 363.9 jit_solution(15413979670254158427)
XLA Ops:
  7.2 1.5 fusion.34
  13.2 0.8 slice_multiply_fusion.2
  14.1 6.3 %collective-permute-start = (f32[4,4,1,128]{3,2,1,0:T(1,128)S(1)}, f32[4,4,1,128]{3,2,1,0:T(1,128)S(1)}, u32[]{:S(2)}, u32[]{:S(2)}) collective-permute-start(f32[4,4,1,128]{3,2,1,0:T(1,128)S(1)} %get-tuple-element.29), channel_id=1, source_target_pairs={{0,16},{2,18},{4,20},{6,22},{8,24},{10,26},{12,28},{14,30},{16,32}... | collective-permute-start | bytes 24584 | tf_op jit(solution)/shard_map/ppermute | solution.py:13
  20.4 1.3 collective-permute-start.1
  21.7 1.8 copy_multiply_fusion
  23.6 2.7 collective-permute-done.1
  26.4 5.1 %collective-permute-start.2 = (f32[4,4,10,1]{3,2,1,0:T(8,128)S(1)}, f32[4,4,10,1]{3,2,1,0:T(8,128)S(1)}, u32[]{:S(2)}, u32[]{:S(2)}) collective-permute-start(f32[4,4,10,1]{3,2,1,0:T(8,128)S(1)} %get-tuple-element.27), channel_id=1, source_target_pairs={{0,2},{2,4},{4,6},{6,8},{8,10},{10,12},{12,14},{14,16},{16,18},{18... | collective-permute-start | bytes 1928 | tf_op jit(solution)/shard_map/ppermute | solution.py:13
  31.6 1.9 collective-permute-start.3
  33.5 3.2 collective-permute-start.4
  36.7 1.3 collective-permute-start.5
  38.6 5.3 %collective-permute-done.5 = f32[64,4,1,128]{3,0,2,1:T(8,128)S(1)} collective-permute-done((f32[64,4,1,128]{3,0,2,1:T(8,128)S(1)}, f32[64,4,1,128]{3,0,2,1:T(8,128)S(1)}, u32[]{:S(2)}, u32[]{:S(2)}) %collective-permute-start.5) | collective-permute-done | bytes 131104 | tf_op jit(solution)/shard_map/ppermute | solution.py:13
  44.0 1.5 fusion.28
  45.6 2.0 copy.15
  48.3 8.0 %collective-permute-start.7 = (f32[64,4,10,1]{0,2,3,1:T(8,128)S(1)}, f32[64,4,10,1]{0,2,3,1:T(8,128)S(1)}, u32[]{:S(2)}, u32[]{:S(2)}) collective-permute-start(f32[64,4,10,1]{0,2,3,1:T(8,128)S(1)} %copy.16), channel_id=1, source_target_pairs={{2,0},{4,2},{6,4},{8,6},{10,8},{12,10},{14,12},{16,14},{18,16},{20... | collective-permute-start | bytes 30728 | tf_op jit(solution)/shard_map/ppermute | solution.py:13
  56.2 1.9 collective-permute-start.6
  58.4 1.0 collective-permute-done.6
  59.8 1.6 copy.18
  61.4 2.4 pad_maximum_fusion
  64.6 0.9 copy-done.1
  65.5 0.8 fusion
  66.7 1.3 fusion.23
  68.0 6.0 %collective-permute-start.8 = (f32[64,4,1,128]{3,0,2,1:T(8,128)S(1)}, f32[64,4,1,128]{3,0,2,1:T(8,128)S(1)}, u32[]{:S(2)}, u32[]{:S(2)}) collective-permute-start(f32[64,4,1,128]{3,0,2,1:T(8,128)S(1)} %get-tuple-element.20), channel_id=1, source_target_pairs={{0,16},{2,18},{4,20},{6,22},{8,24},{10,26},{12,28},{14,30},{16,32}... | collective-permute-start | bytes 393224 | tf_op jit(solution)/shard_map/ppermute | solution.py:13
  74.1 1.3 collective-permute-start.9
  76.0 5.3 %collective-permute-done.9 = f32[64,4,1,128]{3,0,2,1:T(8,128)S(1)} collective-permute-done((f32[64,4,1,128]{3,0,2,1:T(8,128)S(1)}, f32[64,4,1,128]{3,0,2,1:T(8,128)S(1)}, u32[]{:S(2)}, u32[]{:S(2)}) %collective-permute-start.9) | collective-permute-done | bytes 131104 | tf_op jit(solution)/shard_map/ppermute | solution.py:13
  81.4 1.5 fusion.27
  82.9 2.0 copy.21
  84.9 5.5 %collective-permute-start.10 = (f32[64,4,10,1]{0,2,3,1:T(8,128)S(1)}, f32[64,4,10,1]{0,2,3,1:T(8,128)S(1)}, u32[]{:S(2)}, u32[]{:S(2)}) collective-permute-start(f32[64,4,10,1]{0,2,3,1:T(8,128)S(1)} %copy.21), channel_id=1, source_target_pairs={{0,2},{2,4},{4,6},{6,8},{8,10},{10,12},{12,14},{14,16},{16,18},{18... | collective-permute-start | bytes 30728 | tf_op jit(solution)/shard_map/ppermute | solution.py:13
  91.1 5.1 %collective-permute-start.11 = (f32[64,4,10,1]{0,2,3,1:T(8,128)S(1)}, f32[64,4,10,1]{0,2,3,1:T(8,128)S(1)}, u32[]{:S(2)}, u32[]{:S(2)}) collective-permute-start(f32[64,4,10,1]{0,2,3,1:T(8,128)S(1)} %copy.22), channel_id=1, source_target_pairs={{2,0},{4,2},{6,4},{8,6},{10,8},{12,10},{14,12},{16,14},{18,16},{20... | collective-permute-start | bytes 30728 | tf_op jit(solution)/shard_map/ppermute | solution.py:13
  96.9 1.6 copy.24
  98.4 2.4 pad_maximum_fusion.1
  101.6 0.9 copy-done.2
  103.3 1.3 fusion.20
  104.7 4.5 %collective-permute-start.12 = (f32[64,4,1,128]{3,0,2,1:T(8,128)S(1)}, f32[64,4,1,128]{3,0,2,1:T(8,128)S(1)}, u32[]{:S(2)}, u32[]{:S(2)}) collective-permute-start(f32[64,4,1,128]{3,0,2,1:T(8,128)S(1)} %get-tuple-element.18), channel_id=1, source_target_pairs={{0,16},{2,18},{4,20},{6,22},{8,24},{10,26},{12,28},{14,30},{16,32}... | collective-permute-start | bytes 393224 | tf_op jit(solution)/shard_map/ppermute | solution.py:13
  109.2 1.3 collective-permute-start.13
  111.1 5.3 %collective-permute-done.13 = f32[64,4,1,128]{3,0,2,1:T(8,128)S(1)} collective-permute-done((f32[64,4,1,128]{3,0,2,1:T(8,128)S(1)}, f32[64,4,1,128]{3,0,2,1:T(8,128)S(1)}, u32[]{:S(2)}, u32[]{:S(2)}) %collective-permute-start.13) | collective-permute-done | bytes 131104 | tf_op jit(solution)/shard_map/ppermute | solution.py:13
  116.5 1.5 fusion.26
  118.0 2.0 copy.27
  120.0 1.9 collective-permute-start.14
  122.6 8.8 %collective-permute-start.15 = (f32[64,4,10,1]{0,2,3,1:T(8,128)S(1)}, f32[64,4,10,1]{0,2,3,1:T(8,128)S(1)}, u32[]{:S(2)}, u32[]{:S(2)}) collective-permute-start(f32[64,4,10,1]{0,2,3,1:T(8,128)S(1)} %copy.28), channel_id=1, source_target_pairs={{2,0},{4,2},{6,4},{8,6},{10,8},{12,10},{14,12},{16,14},{18,16},{20... | collective-permute-start | bytes 30728 | tf_op jit(solution)/shard_map/ppermute | solution.py:13
  132.3 1.6 copy.30
  133.8 2.4 pad_maximum_fusion.2
  137.1 0.9 copy-done.3
  138.8 1.3 fusion.17
  140.1 6.4 %collective-permute-start.16 = (f32[64,4,1,128]{3,0,2,1:T(8,128)S(1)}, f32[64,4,1,128]{3,0,2,1:T(8,128)S(1)}, u32[]{:S(2)}, u32[]{:S(2)}) collective-permute-start(f32[64,4,1,128]{3,0,2,1:T(8,128)S(1)} %get-tuple-element.16), channel_id=1, source_target_pairs={{0,16},{2,18},{4,20},{6,22},{8,24},{10,26},{12,28},{14,30},{16,32}... | collective-permute-start | bytes 393224 | tf_op jit(solution)/shard_map/ppermute | solution.py:13
  146.5 1.3 collective-permute-start.17
  148.4 5.3 %collective-permute-done.17 = f32[64,4,1,128]{3,0,2,1:T(8,128)S(1)} collective-permute-done((f32[64,4,1,128]{3,0,2,1:T(8,128)S(1)}, f32[64,4,1,128]{3,0,2,1:T(8,128)S(1)}, u32[]{:S(2)}, u32[]{:S(2)}) %collective-permute-start.17) | collective-permute-done | bytes 131104 | tf_op jit(solution)/shard_map/ppermute | solution.py:13
  153.8 1.5 fusion.25
  155.3 2.0 copy.33
  157.3 1.9 collective-permute-start.18
  159.9 9.0 %collective-permute-start.19 = (f32[64,4,10,1]{0,2,3,1:T(8,128)S(1)}, f32[64,4,10,1]{0,2,3,1:T(8,128)S(1)}, u32[]{:S(2)}, u32[]{:S(2)}) collective-permute-start(f32[64,4,10,1]{0,2,3,1:T(8,128)S(1)} %copy.34), channel_id=1, source_target_pairs={{2,0},{4,2},{6,4},{8,6},{10,8},{12,10},{14,12},{16,14},{18,16},{20... | collective-permute-start | bytes 30728 | tf_op jit(solution)/shard_map/ppermute | solution.py:13
  169.6 1.6 copy.36
  171.1 2.4 pad_maximum_fusion.3
  174.3 0.9 copy-done
  176.0 1.3 fusion.14
  178.0 15.8 %all_to_all.15 = f32[64,4,8,128]{3,2,0,1:T(8,128)S(1)} all-to-all(f32[64,4,8,128]{3,2,0,1:T(8,128)S(1)} %copy.39), channel_id=1, replica_groups=mesh['tiles'=64,'vec'=2] {'vec'}, dimensions={1} | all-to-all | bytes 2097152 | tf_op jit(solution)/shard_map/all_to_all | solution.py:80
  193.8 1.1 copy.52
  194.9 1.4 reshape.96
  196.3 1.1 mul.184
  197.5 2.9 convolution_multiply_fusion
  200.3 1.6 copy.43
  201.9 139.6 %all-reduce.10.cloned.1.call-done = f32[128,128]{0,1:T(8,128)} async-done(((f32[128,128]{0,1:T(8,128)}), f32[128,128]{0,1:T(8,128)}) %all-reduce.10.cloned.1.call-update) | async-done | bytes 65552 | tf_op jit(solution)/shard_map/psum | solution.py:95
  341.5 0.9 copy.42
  342.4 0.9 fusion.24
  343.3 11.7 %cholesky.18 = f32[128,128]{1,0:T(8,128)S(1)} custom-call(f32[128,128]{1,0:T(8,128)S(1)} %fusion.24), custom_call_target="Cholesky" | custom-call | tf_op jit(solution)/shard_map/jit(cholesky)/cholesky | solution.py:96
  (80 shorter events, 19.2 us)
Async XLA Ops:
  7.2 334.3 %all-reduce.10.cloned.1.call-start = ((), (), s32[]{:S(2)}) async-start(), calls=%async_computation.1 | async-start | bytes 131072 | tf_op jit(solution)/shard_map/psum | solution.py:95
  14.1 9.5 %collective-permute-start = (f32[4,4,1,128]{3,2,1,0:T(1,128)S(1)}, f32[4,4,1,128]{3,2,1,0:T(1,128)S(1)}, u32[]{:S(2)}, u32[]{:S(2)}) collective-permute-start(f32[4,4,1,128]{3,2,1,0:T(1,128)S(1)} %get-tuple-element.29), channel_id=1, source_target_pairs={{0,16},{2,18},{4,20},{6,22},{8,24},{10,26},{12,28},{14,30},{16,32}... | collective-permute-start | bytes 24584 | tf_op jit(solution)/shard_map/ppermute | solution.py:13
  20.4 5.9 %collective-permute-start.1 = (f32[4,4,1,128]{3,2,1,0:T(1,128)S(1)}, f32[4,4,1,128]{3,2,1,0:T(1,128)S(1)}, u32[]{:S(2)}, u32[]{:S(2)}) collective-permute-start(f32[4,4,1,128]{3,2,1,0:T(1,128)S(1)} %get-tuple-element.30), channel_id=1, source_target_pairs={{16,0},{18,2},{20,4},{22,6},{24,8},{26,10},{28,12},{30,14},{32,16}... | collective-permute-start | bytes 24584 | tf_op jit(solution)/shard_map/ppermute | solution.py:13
  26.4 11.6 %collective-permute-start.2 = (f32[4,4,10,1]{3,2,1,0:T(8,128)S(1)}, f32[4,4,10,1]{3,2,1,0:T(8,128)S(1)}, u32[]{:S(2)}, u32[]{:S(2)}) collective-permute-start(f32[4,4,10,1]{3,2,1,0:T(8,128)S(1)} %get-tuple-element.27), channel_id=1, source_target_pairs={{0,2},{2,4},{4,6},{6,8},{8,10},{10,12},{12,14},{14,16},{16,18},{18... | collective-permute-start | bytes 1928 | tf_op jit(solution)/shard_map/ppermute | solution.py:13
  31.6 6.5 %collective-permute-start.3 = (f32[4,4,10,1]{3,2,1,0:T(8,128)S(1)}, f32[4,4,10,1]{3,2,1,0:T(8,128)S(1)}, u32[]{:S(2)}, u32[]{:S(2)}) collective-permute-start(f32[4,4,10,1]{3,2,1,0:T(8,128)S(1)} %get-tuple-element.28), channel_id=1, source_target_pairs={{2,0},{4,2},{6,4},{8,6},{10,8},{12,10},{14,12},{16,14},{18,16},{20... | collective-permute-start | bytes 1928 | tf_op jit(solution)/shard_map/ppermute | solution.py:13
  33.5 5.1 %collective-permute-start.4 = (f32[64,4,1,128]{3,0,2,1:T(8,128)S(1)}, f32[64,4,1,128]{3,0,2,1:T(8,128)S(1)}, u32[]{:S(2)}, u32[]{:S(2)}) collective-permute-start(f32[64,4,1,128]{3,0,2,1:T(8,128)S(1)} %get-tuple-element.22), channel_id=1, source_target_pairs={{0,16},{2,18},{4,20},{6,22},{8,24},{10,26},{12,28},{14,30},{16,32}... | collective-permute-start | bytes 393224 | tf_op jit(solution)/shard_map/ppermute | solution.py:13
  36.7 7.2 %collective-permute-start.5 = (f32[64,4,1,128]{3,0,2,1:T(8,128)S(1)}, f32[64,4,1,128]{3,0,2,1:T(8,128)S(1)}, u32[]{:S(2)}, u32[]{:S(2)}) collective-permute-start(f32[64,4,1,128]{3,0,2,1:T(8,128)S(1)} %get-tuple-element.23), channel_id=1, source_target_pairs={{16,0},{18,2},{20,4},{22,6},{24,8},{26,10},{28,12},{30,14},{32,16}... | collective-permute-start | bytes 393224 | tf_op jit(solution)/shard_map/ppermute | solution.py:13
  48.3 11.5 %collective-permute-start.7 = (f32[64,4,10,1]{0,2,3,1:T(8,128)S(1)}, f32[64,4,10,1]{0,2,3,1:T(8,128)S(1)}, u32[]{:S(2)}, u32[]{:S(2)}) collective-permute-start(f32[64,4,10,1]{0,2,3,1:T(8,128)S(1)} %copy.16), channel_id=1, source_target_pairs={{2,0},{4,2},{6,4},{8,6},{10,8},{12,10},{14,12},{16,14},{18,16},{20... | collective-permute-start | bytes 30728 | tf_op jit(solution)/shard_map/ppermute | solution.py:13
  56.2 3.1 collective-permute-start.6
  58.2 42.7 %copy-start.5 = (f32[3,10,130]{2,1,0:T(8,128)}, f32[3,10,130]{2,1,0:T(8,128)S(1)}, u32[]{:S(2)}) copy-start(f32[3,10,130]{2,1,0:T(8,128)S(1)} %slice_bitcast_fusion.3) | copy-start | bytes 46804
  64.1 1.3 copy-start.1
  65.5 1.2 copy-start.4
  68.0 8.0 %collective-permute-start.8 = (f32[64,4,1,128]{3,0,2,1:T(8,128)S(1)}, f32[64,4,1,128]{3,0,2,1:T(8,128)S(1)}, u32[]{:S(2)}, u32[]{:S(2)}) collective-permute-start(f32[64,4,1,128]{3,0,2,1:T(8,128)S(1)} %get-tuple-element.20), channel_id=1, source_target_pairs={{0,16},{2,18},{4,20},{6,22},{8,24},{10,26},{12,28},{14,30},{16,32}... | collective-permute-start | bytes 393224 | tf_op jit(solution)/shard_map/ppermute | solution.py:13
  74.1 7.2 %collective-permute-start.9 = (f32[64,4,1,128]{3,0,2,1:T(8,128)S(1)}, f32[64,4,1,128]{3,0,2,1:T(8,128)S(1)}, u32[]{:S(2)}, u32[]{:S(2)}) collective-permute-start(f32[64,4,1,128]{3,0,2,1:T(8,128)S(1)} %get-tuple-element.21), channel_id=1, source_target_pairs={{16,0},{18,2},{20,4},{22,6},{24,8},{26,10},{28,12},{30,14},{32,16}... | collective-permute-start | bytes 393224 | tf_op jit(solution)/shard_map/ppermute | solution.py:13
  84.9 11.3 %collective-permute-start.10 = (f32[64,4,10,1]{0,2,3,1:T(8,128)S(1)}, f32[64,4,10,1]{0,2,3,1:T(8,128)S(1)}, u32[]{:S(2)}, u32[]{:S(2)}) collective-permute-start(f32[64,4,10,1]{0,2,3,1:T(8,128)S(1)} %copy.21), channel_id=1, source_target_pairs={{0,2},{2,4},{4,6},{6,8},{8,10},{10,12},{12,14},{14,16},{16,18},{18... | collective-permute-start | bytes 30728 | tf_op jit(solution)/shard_map/ppermute | solution.py:13
  91.1 5.8 %collective-permute-start.11 = (f32[64,4,10,1]{0,2,3,1:T(8,128)S(1)}, f32[64,4,10,1]{0,2,3,1:T(8,128)S(1)}, u32[]{:S(2)}, u32[]{:S(2)}) collective-permute-start(f32[64,4,10,1]{0,2,3,1:T(8,128)S(1)} %copy.22), channel_id=1, source_target_pairs={{2,0},{4,2},{6,4},{8,6},{10,8},{12,10},{14,12},{16,14},{18,16},{20... | collective-permute-start | bytes 30728 | tf_op jit(solution)/shard_map/ppermute | solution.py:13
  101.2 1.3 copy-start.2
  104.7 6.4 %collective-permute-start.12 = (f32[64,4,1,128]{3,0,2,1:T(8,128)S(1)}, f32[64,4,1,128]{3,0,2,1:T(8,128)S(1)}, u32[]{:S(2)}, u32[]{:S(2)}) collective-permute-start(f32[64,4,1,128]{3,0,2,1:T(8,128)S(1)} %get-tuple-element.18), channel_id=1, source_target_pairs={{0,16},{2,18},{4,20},{6,22},{8,24},{10,26},{12,28},{14,30},{16,32}... | collective-permute-start | bytes 393224 | tf_op jit(solution)/shard_map/ppermute | solution.py:13
  109.2 7.2 %collective-permute-start.13 = (f32[64,4,1,128]{3,0,2,1:T(8,128)S(1)}, f32[64,4,1,128]{3,0,2,1:T(8,128)S(1)}, u32[]{:S(2)}, u32[]{:S(2)}) collective-permute-start(f32[64,4,1,128]{3,0,2,1:T(8,128)S(1)} %get-tuple-element.19), channel_id=1, source_target_pairs={{16,0},{18,2},{20,4},{22,6},{24,8},{26,10},{28,12},{30,14},{32,16}... | collective-permute-start | bytes 393224 | tf_op jit(solution)/shard_map/ppermute | solution.py:13
  120.0 11.4 %collective-permute-start.14 = (f32[64,4,10,1]{0,2,3,1:T(8,128)S(1)}, f32[64,4,10,1]{0,2,3,1:T(8,128)S(1)}, u32[]{:S(2)}, u32[]{:S(2)}) collective-permute-start(f32[64,4,10,1]{0,2,3,1:T(8,128)S(1)} %copy.27), channel_id=1, source_target_pairs={{0,2},{2,4},{4,6},{6,8},{8,10},{10,12},{12,14},{14,16},{16,18},{18... | collective-permute-start | bytes 30728 | tf_op jit(solution)/shard_map/ppermute | solution.py:13
  122.6 9.6 %collective-permute-start.15 = (f32[64,4,10,1]{0,2,3,1:T(8,128)S(1)}, f32[64,4,10,1]{0,2,3,1:T(8,128)S(1)}, u32[]{:S(2)}, u32[]{:S(2)}) collective-permute-start(f32[64,4,10,1]{0,2,3,1:T(8,128)S(1)} %copy.28), channel_id=1, source_target_pairs={{2,0},{4,2},{6,4},{8,6},{10,8},{12,10},{14,12},{16,14},{18,16},{20... | collective-permute-start | bytes 30728 | tf_op jit(solution)/shard_map/ppermute | solution.py:13
  133.8 2.4 copy-start.6
  136.6 1.3 copy-start.3
  140.1 8.3 %collective-permute-start.16 = (f32[64,4,1,128]{3,0,2,1:T(8,128)S(1)}, f32[64,4,1,128]{3,0,2,1:T(8,128)S(1)}, u32[]{:S(2)}, u32[]{:S(2)}) collective-permute-start(f32[64,4,1,128]{3,0,2,1:T(8,128)S(1)} %get-tuple-element.16), channel_id=1, source_target_pairs={{0,16},{2,18},{4,20},{6,22},{8,24},{10,26},{12,28},{14,30},{16,32}... | collective-permute-start | bytes 393224 | tf_op jit(solution)/shard_map/ppermute | solution.py:13
  146.5 7.2 %collective-permute-start.17 = (f32[64,4,1,128]{3,0,2,1:T(8,128)S(1)}, f32[64,4,1,128]{3,0,2,1:T(8,128)S(1)}, u32[]{:S(2)}, u32[]{:S(2)}) collective-permute-start(f32[64,4,1,128]{3,0,2,1:T(8,128)S(1)} %get-tuple-element.17), channel_id=1, source_target_pairs={{16,0},{18,2},{20,4},{22,6},{24,8},{26,10},{28,12},{30,14},{32,16}... | collective-permute-start | bytes 393224 | tf_op jit(solution)/shard_map/ppermute | solution.py:13
  157.3 11.7 %collective-permute-start.18 = (f32[64,4,10,1]{0,2,3,1:T(8,128)S(1)}, f32[64,4,10,1]{0,2,3,1:T(8,128)S(1)}, u32[]{:S(2)}, u32[]{:S(2)}) collective-permute-start(f32[64,4,10,1]{0,2,3,1:T(8,128)S(1)} %copy.33), channel_id=1, source_target_pairs={{0,2},{2,4},{4,6},{6,8},{8,10},{10,12},{12,14},{14,16},{16,18},{18... | collective-permute-start | bytes 30728 | tf_op jit(solution)/shard_map/ppermute | solution.py:13
  159.9 9.6 %collective-permute-start.19 = (f32[64,4,10,1]{0,2,3,1:T(8,128)S(1)}, f32[64,4,10,1]{0,2,3,1:T(8,128)S(1)}, u32[]{:S(2)}, u32[]{:S(2)}) collective-permute-start(f32[64,4,10,1]{0,2,3,1:T(8,128)S(1)} %copy.34), channel_id=1, source_target_pairs={{2,0},{4,2},{6,4},{8,6},{10,8},{12,10},{14,12},{16,14},{18,16},{20... | collective-permute-start | bytes 30728 | tf_op jit(solution)/shard_map/ppermute | solution.py:13
  171.1 2.4 copy-start.7
  173.9 1.3 copy-start
  178.0 16.9 %copy-start.8 = (f32[8,128]{1,0:T(8,128)S(1)}, f32[8,128]{1,0:T(8,128)}, u32[]{:S(2)}) copy-start(f32[8,128]{1,0:T(8,128)} %param.8) | copy-start | bytes 12292
Sparse Core Ops, SparseCore 0:
  200.5 140.9 all-reduce.9
where the time goes:
time: 365 us; the launch traced here: 364 us
  waiting for transfers between devices  167 us (46%)
  starting transfers between devices  82.1 us (22%)
  other arithmetic  40.4 us (11%)
  local copies, waits for them, and re-layouts  38.2 us (10%)
  between operations  17.2 us (5%)
  blocking collectives  15.8 us (4%)
    psum x1, waiting for transfers between devices, shards(): gram = lax.psum(gram_local, ('tiles', 'vec'))  140 us
    ppermute x20, starting transfers between devices, shifted(): lax.ppermute(value, axis, [(source, source + steps) for source in range(f...  82 us
    ppermute x20, waiting for transfers between devices, shifted(): lax.ppermute(value, axis, [(source, source + steps) for source in range(f...  27.8 us
    all_to_all x1, blocking collectives, shards(): lax.all_to_all(field, 'vec', split_axis=1, concat_axis=0, tiled=True)  15.8 us
    slice x9, local copies, waits for them, and re-layouts, extend(): left_rim = neighbour(stacked[:, :, :, -margin:], 1)  14.2 us
    another operation x3, other arithmetic, shards(): r_factor = jnp.linalg.cholesky(gram).T  12.4 us
    concatenate x5, other arithmetic, extend(): return jnp.concatenate([left_rim, stacked, right_rim], axis=3)  9.82 us
    ppermute x8, local copies, waits for them, and re-layouts, shifted(): lax.ppermute(value, axis, [(source, source + steps) for source in range(f...  8.08 us
  transfers between devices with their start and end apart: 21, of which 14 were waited for; matrix products, arithmetic and copies ran while one was open for 2% of the time, Pallas kernels for 0%

commit v1 on v0

--- a/solution.py
+++ b/solution.py
@@ -92,7 +92,9 @@
         )
         / total_cells
     )
-    gram = lax.psum(gram_local, ("tiles", "vec"))
+    gram = gram_local
+    for jj in ("tiles", "vec"):
+        gram = jax.lax.psum(gram, jj)
     r_factor = jnp.linalg.cholesky(gram).T
     return (field, r_factor)
 

time: 365 us -> 817 us (2.24)
  waiting for transfers between devices: 167 us -> 619 us
    psum x1 -> x2, waiting for transfers between devices: 140 us -> 592 us  [shards(): gram = jax.lax.psum(gram, jj)]
  transfers between devices with their start and end apart: 21 -> 22, of which waited for: 14 -> 15; matrix products, arithmetic and copies ran while one was open for 2% -> 1% of each run, Pallas kernels for 0% -> 0%
where the time goes in v1:
time: 817 us; the launch traced here: 816 us
  waiting for transfers between devices  619 us (76%)
  starting transfers between devices  82.1 us (10%)
  other arithmetic  40.4 us (5%)
  local copies, waits for them, and re-layouts  38.2 us (5%)
  between operations  17.2 us (2%)
  blocking collectives  15.8 us (2%)
    psum x2, waiting for transfers between devices, shards(): gram = jax.lax.psum(gram, jj)  592 us
    ppermute x20, starting transfers between devices, shifted(): lax.ppermute(value, axis, [(source, source + steps) for source in range(f...  82 us
    ppermute x20, waiting for transfers between devices, shifted(): lax.ppermute(value, axis, [(source, source + steps) for source in range(f...  27.8 us
  transfers between devices with their start and end apart: 22, of which 15 were waited for; matrix products, arithmetic and copies ran while one was open for 1% of the time, Pallas kernels for 0%

profile of v1, /device:TPU:1, one launch (start us, length us, event | category | flops | bytes accessed | tf_op | source)
XLA Modules:
  0.0 816.0 jit_solution(3874081718535081895)
XLA Ops:
  7.2 1.5 fusion.34
  13.2 0.8 slice_multiply_fusion.2
  14.1 6.3 collective-permute-start
  20.4 1.3 collective-permute-start.1
  21.7 1.8 copy_multiply_fusion
  23.6 2.7 collective-permute-done.1
  26.4 5.1 collective-permute-start.2
  31.6 1.9 collective-permute-start.3
  33.5 3.2 collective-permute-start.4
  36.7 1.3 collective-permute-start.5
  38.6 5.3 collective-permute-done.5
  44.0 1.5 fusion.28
  45.6 2.0 copy.15
  48.3 8.0 collective-permute-start.7
  56.2 1.9 collective-permute-start.6
  58.4 1.0 collective-permute-done.6
  59.8 1.6 copy.18
  61.4 2.4 pad_maximum_fusion
  64.6 0.9 copy-done.1
  66.7 1.3 fusion.23
  68.0 6.0 collective-permute-start.8
  74.1 1.3 collective-permute-start.9
  76.0 5.3 collective-permute-done.9
  81.4 1.5 fusion.27
  82.9 2.0 copy.21
  84.9 5.5 collective-permute-start.10
  91.1 5.1 collective-permute-start.11
  96.9 1.6 copy.24
  98.4 2.4 pad_maximum_fusion.1
  101.6 0.9 copy-done.2
  103.3 1.3 fusion.20
  104.7 4.5 collective-permute-start.12
  109.2 1.3 collective-permute-start.13
  111.1 5.3 collective-permute-done.13
  116.5 1.5 fusion.26
  118.0 2.0 copy.27
  120.0 1.9 collective-permute-start.14
  122.6 8.8 %collective-permute-start.15 = (f32[64,4,10,1]{0,2,3,1:T(8,128)S(1)}, f32[64,4,10,1]{0,2,3,1:T(8,128)S(1)}, u32[]{:S(2)}, u32[]{:S(2)}) collective-permute-start(f32[64,4,10,1]{0,2,3,1:T(8,128)S(1)} %copy.28), channel_id=1, source_target_pairs={{2,0},{4,2},{6,4},{8,6},{10,8},{12,10},{14,12},{16,14},{18,16},{20... | collective-permute-start | bytes 30728 | tf_op jit(solution)/shard_map/ppermute | solution.py:13
  132.3 1.6 copy.30
  133.8 2.4 pad_maximum_fusion.2
  137.1 0.9 copy-done.3
  138.8 1.3 fusion.17
  140.1 6.4 collective-permute-start.16
  146.5 1.3 collective-permute-start.17
  148.4 5.3 collective-permute-done.17
  153.8 1.5 fusion.25
  155.3 2.0 copy.33
  157.3 1.9 collective-permute-start.18
  159.9 9.0 %collective-permute-start.19 = (f32[64,4,10,1]{0,2,3,1:T(8,128)S(1)}, f32[64,4,10,1]{0,2,3,1:T(8,128)S(1)}, u32[]{:S(2)}, u32[]{:S(2)}) collective-permute-start(f32[64,4,10,1]{0,2,3,1:T(8,128)S(1)} %copy.34), channel_id=1, source_target_pairs={{2,0},{4,2},{6,4},{8,6},{10,8},{12,10},{14,12},{16,14},{18,16},{20... | collective-permute-start | bytes 30728 | tf_op jit(solution)/shard_map/ppermute | solution.py:13
  169.6 1.6 copy.36
  171.1 2.4 pad_maximum_fusion.3
  174.3 0.9 copy-done
  176.0 1.3 fusion.14
  178.0 15.8 %all_to_all.15 = f32[64,4,8,128]{3,2,0,1:T(8,128)S(1)} all-to-all(f32[64,4,8,128]{3,2,0,1:T(8,128)S(1)} %copy.39), channel_id=1, replica_groups=mesh['tiles'=64,'vec'=2] {'vec'}, dimensions={1} | all-to-all | bytes 2097152 | tf_op jit(solution)/shard_map/all_to_all | solution.py:80
  193.8 1.1 copy.52
  194.9 1.4 reshape.96
  196.3 1.1 mul.184
  197.5 2.9 convolution_multiply_fusion
  200.4 564.2 %all-reduce.11.cloned.1.call-done = f32[128,128]{0,1:T(8,128)} async-done(((f32[128,128]{0,1:T(8,128)}), f32[128,128]{0,1:T(8,128)}) %all-reduce.11.cloned.1.call-update) | async-done | bytes 65552 | tf_op jit(solution)/shard_map/psum | solution.py:97
  764.6 1.6 copy.43
  766.2 27.4 %all-reduce.13.cloned.1.call-done = f32[128,128]{0,1:T(8,128)} async-done(((f32[128,128]{0,1:T(8,128)}), f32[128,128]{0,1:T(8,128)}) %all-reduce.13.cloned.1.call-update) | async-done | bytes 65552 | tf_op jit(solution)/shard_map/psum | solution.py:97
  793.6 0.9 copy.42
  794.5 0.9 fusion.24
  795.4 11.7 %cholesky.18 = f32[128,128]{1,0:T(8,128)S(1)} custom-call(f32[128,128]{1,0:T(8,128)S(1)} %fusion.24), custom_call_target="Cholesky" | custom-call | tf_op jit(solution)/shard_map/jit(cholesky)/cholesky | solution.py:98
  (83 shorter events, 20.1 us)
Async XLA Ops:
  7.2 757.5 %all-reduce.11.cloned.1.call-start = ((), (), s32[]{:S(2)}) async-start(), calls=%async_computation.1 | async-start | bytes 131072 | tf_op jit(solution)/shard_map/psum | solution.py:97
  14.1 9.5 %collective-permute-start = (f32[4,4,1,128]{3,2,1,0:T(1,128)S(1)}, f32[4,4,1,128]{3,2,1,0:T(1,128)S(1)}, u32[]{:S(2)}, u32[]{:S(2)}) collective-permute-start(f32[4,4,1,128]{3,2,1,0:T(1,128)S(1)} %get-tuple-element.29), channel_id=1, source_target_pairs={{0,16},{2,18},{4,20},{6,22},{8,24},{10,26},{12,28},{14,30},{16,32}... | collective-permute-start | bytes 24584 | tf_op jit(solution)/shard_map/ppermute | solution.py:13
  20.4 5.9 collective-permute-start.1
  26.4 11.6 %collective-permute-start.2 = (f32[4,4,10,1]{3,2,1,0:T(8,128)S(1)}, f32[4,4,10,1]{3,2,1,0:T(8,128)S(1)}, u32[]{:S(2)}, u32[]{:S(2)}) collective-permute-start(f32[4,4,10,1]{3,2,1,0:T(8,128)S(1)} %get-tuple-element.27), channel_id=1, source_target_pairs={{0,2},{2,4},{4,6},{6,8},{8,10},{10,12},{12,14},{14,16},{16,18},{18... | collective-permute-start | bytes 1928 | tf_op jit(solution)/shard_map/ppermute | solution.py:13
  31.6 6.5 collective-permute-start.3
  33.5 5.1 collective-permute-start.4
  36.7 7.2 collective-permute-start.5
  48.3 11.5 %collective-permute-start.7 = (f32[64,4,10,1]{0,2,3,1:T(8,128)S(1)}, f32[64,4,10,1]{0,2,3,1:T(8,128)S(1)}, u32[]{:S(2)}, u32[]{:S(2)}) collective-permute-start(f32[64,4,10,1]{0,2,3,1:T(8,128)S(1)} %copy.16), channel_id=1, source_target_pairs={{2,0},{4,2},{6,4},{8,6},{10,8},{12,10},{14,12},{16,14},{18,16},{20... | collective-permute-start | bytes 30728 | tf_op jit(solution)/shard_map/ppermute | solution.py:13
  56.2 3.1 collective-permute-start.6
  58.2 42.7 %copy-start.5 = (f32[3,10,130]{2,1,0:T(8,128)}, f32[3,10,130]{2,1,0:T(8,128)S(1)}, u32[]{:S(2)}) copy-start(f32[3,10,130]{2,1,0:T(8,128)S(1)} %slice_bitcast_fusion.3) | copy-start | bytes 46804
  64.1 1.3 copy-start.1
  65.5 1.2 copy-start.4
  68.0 8.0 collective-permute-start.8
  74.1 7.2 collective-permute-start.9
  84.9 11.3 %collective-permute-start.10 = (f32[64,4,10,1]{0,2,3,1:T(8,128)S(1)}, f32[64,4,10,1]{0,2,3,1:T(8,128)S(1)}, u32[]{:S(2)}, u32[]{:S(2)}) collective-permute-start(f32[64,4,10,1]{0,2,3,1:T(8,128)S(1)} %copy.21), channel_id=1, source_target_pairs={{0,2},{2,4},{4,6},{6,8},{8,10},{10,12},{12,14},{14,16},{16,18},{18... | collective-permute-start | bytes 30728 | tf_op jit(solution)/shard_map/ppermute | solution.py:13
  91.1 5.8 collective-permute-start.11
  101.2 1.3 copy-start.2
  104.7 6.4 collective-permute-start.12
  109.2 7.2 collective-permute-start.13
  120.0 11.4 %collective-permute-start.14 = (f32[64,4,10,1]{0,2,3,1:T(8,128)S(1)}, f32[64,4,10,1]{0,2,3,1:T(8,128)S(1)}, u32[]{:S(2)}, u32[]{:S(2)}) collective-permute-start(f32[64,4,10,1]{0,2,3,1:T(8,128)S(1)} %copy.27), channel_id=1, source_target_pairs={{0,2},{2,4},{4,6},{6,8},{8,10},{10,12},{12,14},{14,16},{16,18},{18... | collective-permute-start | bytes 30728 | tf_op jit(solution)/shard_map/ppermute | solution.py:13
  122.6 9.6 %collective-permute-start.15 = (f32[64,4,10,1]{0,2,3,1:T(8,128)S(1)}, f32[64,4,10,1]{0,2,3,1:T(8,128)S(1)}, u32[]{:S(2)}, u32[]{:S(2)}) collective-permute-start(f32[64,4,10,1]{0,2,3,1:T(8,128)S(1)} %copy.28), channel_id=1, source_target_pairs={{2,0},{4,2},{6,4},{8,6},{10,8},{12,10},{14,12},{16,14},{18,16},{20... | collective-permute-start | bytes 30728 | tf_op jit(solution)/shard_map/ppermute | solution.py:13
  133.8 2.4 copy-start.6
  136.6 1.3 copy-start.3
  140.1 8.3 %collective-permute-start.16 = (f32[64,4,1,128]{3,0,2,1:T(8,128)S(1)}, f32[64,4,1,128]{3,0,2,1:T(8,128)S(1)}, u32[]{:S(2)}, u32[]{:S(2)}) collective-permute-start(f32[64,4,1,128]{3,0,2,1:T(8,128)S(1)} %get-tuple-element.16), channel_id=1, source_target_pairs={{0,16},{2,18},{4,20},{6,22},{8,24},{10,26},{12,28},{14,30},{16,32}... | collective-permute-start | bytes 393224 | tf_op jit(solution)/shard_map/ppermute | solution.py:13
  146.5 7.2 collective-permute-start.17
  157.3 11.7 %collective-permute-start.18 = (f32[64,4,10,1]{0,2,3,1:T(8,128)S(1)}, f32[64,4,10,1]{0,2,3,1:T(8,128)S(1)}, u32[]{:S(2)}, u32[]{:S(2)}) collective-permute-start(f32[64,4,10,1]{0,2,3,1:T(8,128)S(1)} %copy.33), channel_id=1, source_target_pairs={{0,2},{2,4},{4,6},{6,8},{8,10},{10,12},{12,14},{14,16},{16,18},{18... | collective-permute-start | bytes 30728 | tf_op jit(solution)/shard_map/ppermute | solution.py:13
  159.9 9.6 %collective-permute-start.19 = (f32[64,4,10,1]{0,2,3,1:T(8,128)S(1)}, f32[64,4,10,1]{0,2,3,1:T(8,128)S(1)}, u32[]{:S(2)}, u32[]{:S(2)}) collective-permute-start(f32[64,4,10,1]{0,2,3,1:T(8,128)S(1)} %copy.34), channel_id=1, source_target_pairs={{2,0},{4,2},{6,4},{8,6},{10,8},{12,10},{14,12},{16,14},{18,16},{20... | collective-permute-start | bytes 30728 | tf_op jit(solution)/shard_map/ppermute | solution.py:13
  171.1 2.4 copy-start.7
  173.9 1.3 copy-start
  178.0 16.9 %copy-start.8 = (f32[8,128]{1,0:T(8,128)S(1)}, f32[8,128]{1,0:T(8,128)}, u32[]{:S(2)}) copy-start(f32[8,128]{1,0:T(8,128)} %param.8) | copy-start | bytes 12292
  200.3 593.3 %all-reduce.13.cloned.1.call-start = ((), (), s32[]{:S(2)}) async-start(), calls=%async_computation.2 | async-start | bytes 131072 | tf_op jit(solution)/shard_map/psum | solution.py:97
Sparse Core Ops, SparseCore 0:
  200.5 564.1 all-reduce.10
  767.0 26.5 all-reduce.12
